TPU v7x, 32 devices: a whole 2x2x4 slice. The times are simulated.
32 devices in a mesh: grp: 4 (over y, core), dev: 8 (over z, x).
Axes of the slice: x: 2, y: 2, z: 4, core: 2. Of those that a mesh axis runs over, the one named last changes fastest.
Arguments:
- visibilities: bfloat16 [16384, 2, 128], P(('grp', 'dev')), may hold values from -6 to 6
- owner: int32 [16384, 1], P(('grp', 'dev')), may hold values from 0 to 31; in each aligned block of 512 rows (0 to 511, 512 to 1023, ...) at most 32 rows name the same one
- tile_slot: int32 [16384], P(('grp', 'dev')), may hold values from 0 to 511
- kernel_index: int32 [16384, 2], P(('grp', 'dev')), may hold values from 0 to 31
- kernels: bfloat16 [2, 32, 64, 128], replicated, may hold values from -1 to 1
Outputs:
- image: float32 [2, 8192, 8192], P(None, ('grp', 'dev'))
Inputs may be any that keep to these rules, and one draw needn't show every extreme that they name: owner[r, 0] = g * 8 + d names group g and owner d; among the rows of one device no owner is named by more than 32 rows, a bound that some block reaches.
All inputs are finite; a program needn't handle non-finite values.
Results may differ from a plain program's by a relative error of at most 0.0029.
Values may be sent and summed in bfloat16 or wider, within the bound.
A program may use at most 128 MiB of HBM per device.

v0:
```python
import math
import jax
import jax.numpy as jnp
from jax import lax
from jax.sharding import PartitionSpec as P

GRID = 8192
TILE = 64
VIS = 128
QLEN = 128


def complex_product(pattern, left_re, left_im, right_re, right_im):

    def product(first, second):
        return jnp.einsum(pattern, first, second, precision=lax.Precision.HIGHEST)

    return (
        product(left_re, right_re) - product(left_im, right_im),
        product(left_re, right_im) + product(left_im, right_re),
    )


def phase_table(first, second, modulus):
    angle = (
        2.0 * math.pi / modulus * (first[:, None] * second[None, :] % modulus).astype(jnp.float32)
    )
    return (jnp.cos(angle), jnp.sin(angle))


def along_rows(field):
    lines = field.shape[1]
    plen = GRID // QLEN
    outer_idx = jnp.arange(QLEN, dtype=jnp.int32)
    inner_idx = jnp.arange(plen, dtype=jnp.int32)
    outer_re, outer_im = phase_table(outer_idx, outer_idx, QLEN)
    turn_re, turn_im = phase_table(outer_idx, inner_idx, GRID)
    inner_re, inner_im = phase_table(inner_idx, inner_idx, plen)
    field_re = field[0].reshape(lines, QLEN, plen)
    field_im = field[1].reshape(lines, QLEN, plen)
    middle_re, middle_im = complex_product("kq,rqp->rkp", outer_re, outer_im, field_re, field_im)
    middle_re, middle_im = (
        middle_re * turn_re - middle_im * turn_im,
        middle_re * turn_im + middle_im * turn_re,
    )
    result_re, result_im = complex_product("rkp,pb->rbk", middle_re, middle_im, inner_re, inner_im)
    return jnp.stack([result_re.reshape(lines, GRID), result_im.reshape(lines, GRID)])


def along_columns(field, source_order):
    width = field.shape[2]
    plen = GRID // QLEN
    outer_idx = jnp.arange(QLEN, dtype=jnp.int32)
    inner_idx = jnp.arange(plen, dtype=jnp.int32)
    outer_re, outer_im = phase_table(outer_idx, source_order, QLEN)
    turn_re, turn_im = phase_table(outer_idx, inner_idx, GRID)
    inner_re, inner_im = phase_table(inner_idx, inner_idx, plen)
    field_re = field[0].reshape(QLEN, plen, width)
    field_im = field[1].reshape(QLEN, plen, width)
    middle_re, middle_im = complex_product("bk,kpa->bpa", outer_re, outer_im, field_re, field_im)
    turn_re = turn_re[:, :, None]
    turn_im = turn_im[:, :, None]
    middle_re, middle_im = (
        middle_re * turn_re - middle_im * turn_im,
        middle_re * turn_im + middle_im * turn_re,
    )
    result_re, result_im = complex_product("kpa,pb->abk", middle_re, middle_im, inner_re, inner_im)
    scale = 1.0 / GRID
    return jnp.stack(
        [result_re.reshape(width, GRID) * scale, result_im.reshape(width, GRID) * scale]
    )


def local(visibilities, owner, tile_slot, kernel_index, kernels):
    groups = lax.axis_size("grp")
    owners = lax.axis_size("dev")
    devices = groups * owners
    rows_here = visibilities.shape[0]
    capacity = 2 * rows_here // devices
    target = owner[:, 0]
    onehot = (target[:, None] == jnp.arange(devices, dtype=jnp.int32)[None, :]).astype(jnp.int32)
    slot_rank = jnp.sum((jnp.cumsum(onehot, axis=0) - 1) * onehot, axis=1)
    position = target * capacity + slot_rank
    total_rows = devices * capacity
    vis_out = jnp.zeros((total_rows, 2, VIS), jnp.bfloat16).at[position].set(visibilities)
    labels = jnp.concatenate([tile_slot[:, None], kernel_index], axis=1)
    label_out = jnp.zeros((total_rows, 3), jnp.int32).at[position].set(labels)
    vis_in, label_in = (
        lax.all_to_all(
            vis_out.reshape(devices, capacity, 2, VIS),
            ("grp", "dev"),
            split_axis=0,
            concat_axis=0,
            tiled=True,
        ),
        lax.all_to_all(
            label_out.reshape(devices, capacity, 3),
            ("grp", "dev"),
            split_axis=0,
            concat_axis=0,
            tiled=True,
        ),
    )
    vis_in = vis_in.reshape(total_rows, 2, VIS)
    label_in = label_in.reshape(total_rows, 3)
    slab = GRID // devices
    tile_rows = slab // TILE
    tile_cols = GRID // TILE
    block_rows = min(256, total_rows)
    block_count = total_rows // block_rows

    def grid_block(block_index, uv_tiles):
        first_row = block_index * block_rows
        vis_block = lax.dynamic_slice_in_dim(vis_in, first_row, block_rows, 0)
        label_block = lax.dynamic_slice_in_dim(label_in, first_row, block_rows, 0)
        left_kernel = jnp.take(kernels[0], label_block[:, 1], axis=0)
        right_kernel = jnp.take(kernels[1], label_block[:, 2], axis=0)
        weighted = (
            left_kernel.astype(jnp.float32)[:, None, :, :]
            * vis_block.astype(jnp.float32)[:, :, None, :]
        ).astype(jnp.bfloat16)
        terms = jnp.einsum(
            "rcik,rjk->rcij", weighted, right_kernel, preferred_element_type=jnp.float32
        )
        return uv_tiles.at[label_block[:, 0]].add(terms)

    empty = jnp.zeros((tile_rows * tile_cols, 2, TILE, TILE), jnp.float32)
    uv_tiles = lax.fori_loop(0, block_count, grid_block, empty)
    grid_rows = uv_tiles.reshape(tile_rows, tile_cols, 2, TILE, TILE).transpose(2, 0, 3, 1, 4)
    grid_rows = grid_rows.reshape(2, slab, GRID)
    half = along_rows(grid_rows)
    columns = lax.all_to_all(half, ("grp", "dev"), split_axis=2, concat_axis=1, tiled=True)
    source_order = jnp.arange(QLEN, dtype=jnp.int32)
    return along_columns(columns, source_order)


def solution(mesh):
    return jax.shard_map(
        local,
        mesh=mesh,
        in_specs=(
            P(("grp", "dev"), None, None),
            P(("grp", "dev"), None),
            P(("grp", "dev")),
            P(("grp", "dev"), None),
            P(),
        ),
        out_specs=P(None, ("grp", "dev"), None),
        check_vma=False,
    )
```

profile of v0, /device:TPU:0, one launch (start us, length us, event | category | flops | bytes accessed | tf_op | source)
XLA Modules:
  0.0 1191.1 jit_solution(2324823761991537444)
XLA Ops:
  0.7 1.2 reduce-window.6
  2.1 0.8 fusion.48
  4.5 1.8 scatter_custom_fusion.1
  6.3 0.9 copy.83
  7.2 7.3 all-to-all-start
  14.5 1.1 broadcast_in_dim.29
  15.5 49.6 %scatter_fusion.1 = bf16[1024,2,128]{2,1,0:T(2,128)(2,1)} fusion(bf16[1024,2,128]{2,1,0:T(2,128)(2,1)} %broadcast_in_dim.29, s32[512]{0:T(512)S(1)} %bitcast.149, bf16[512,2,128]{2,1,0:T(2,128)(2,1)} %param.9), kind=kCustom, calls=%fused_computation.4 | custom fusion | bytes 788480 | tf_op jit(solution)/shard_map/scatter | solution.py:85
  65.2 6.4 all-to-all-start.1
  71.5 0.8 fusion.95
  72.4 15.5 %all-to-all-done.1 = bf16[32,32,2,128]{3,2,1,0:T(2,128)(2,1)S(1)} async-done(((bf16[32,32,2,128]{3,2,1,0:T(2,128)(2,1)}), bf16[32,32,2,128]{3,2,1,0:T(2,128)(2,1)S(1)}, u32[]{:S(2)}, u32[]{:S(2)}) %all-to-all-start.1) | async-done | bytes 524320 | tf_op jit(solution)/shard_map/all_to_all | solution.py:89
  87.9 11.2 broadcast_in_dim.26
  99.1 297.3 %while.13 = (s32[]{:T(128)}, f32[512,2,64,64]{3,2,1,0:T(8,128)}, s32[1024,3]{0,1:T(4,128)S(1)}, bf16[2,32,64,128]{3,2,1,0:T(8,128)(2,1)S(1)}, bf16[1024,2,128]{2...) while((s32[]{:T(128)}, f32[512,2,64,64]{3,2,1,0:T(8,128)}, ...), condition=%wide.region_7.9_spmd, body=%wide.region_5.0_spmd.sunk | while | flops 553721088 | bytes 78276800 | solution.py:128
  99.3 3.1 gather_fusion
  102.4 5.3 select_convert_fusion.2
  107.7 3.0 gather_fusion.1
  110.8 10.4 fusion.183
  121.2 52.2 %scatter_fusion = f32[512,2,64,64]{3,2,1,0:T(8,128)} fusion(f32[512,2,64,64]{3,2,1,0:T(8,128)} %get-tuple-element.179, s32[256]{0:T(256)S(1)} %bitcast.141, f32[256,2,64,64]{3,2,1,0:T(8,128)} %fusion.183), kind=kCustom, calls=%fused_computation.2.clone.1 | custom fusion | flops 2097152 | bytes 25166848 | tf_op jit(solution)/shard_map/while/body/eval_jaxpr/scatter-add | solution.py:125
  173.6 3.1 gather_fusion
  176.7 5.3 select_convert_fusion.2
  182.0 3.0 gather_fusion.1
  185.1 10.4 fusion.183
  195.5 52.3 %scatter_fusion = f32[512,2,64,64]{3,2,1,0:T(8,128)} fusion(f32[512,2,64,64]{3,2,1,0:T(8,128)} %get-tuple-element.179, s32[256]{0:T(256)S(1)} %bitcast.141, f32[256,2,64,64]{3,2,1,0:T(8,128)} %fusion.183), kind=kCustom, calls=%fused_computation.2.clone.1 | custom fusion | flops 2097152 | bytes 25166848 | tf_op jit(solution)/shard_map/while/body/eval_jaxpr/scatter-add | solution.py:125
  248.0 3.1 gather_fusion
  251.1 5.3 select_convert_fusion.2
  256.4 3.0 gather_fusion.1
  259.5 10.4 fusion.183
  269.9 52.2 %scatter_fusion = f32[512,2,64,64]{3,2,1,0:T(8,128)} fusion(f32[512,2,64,64]{3,2,1,0:T(8,128)} %get-tuple-element.179, s32[256]{0:T(256)S(1)} %bitcast.141, f32[256,2,64,64]{3,2,1,0:T(8,128)} %fusion.183), kind=kCustom, calls=%fused_computation.2.clone.1 | custom fusion | flops 2097152 | bytes 25166848 | tf_op jit(solution)/shard_map/while/body/eval_jaxpr/scatter-add | solution.py:125
  322.2 3.1 gather_fusion
  325.3 5.3 select_convert_fusion.2
  330.6 3.0 gather_fusion.1
  333.8 10.4 fusion.183
  344.1 52.3 %scatter_fusion = f32[512,2,64,64]{3,2,1,0:T(8,128)} fusion(f32[512,2,64,64]{3,2,1,0:T(8,128)} %get-tuple-element.179, s32[256]{0:T(256)S(1)} %bitcast.141, f32[256,2,64,64]{3,2,1,0:T(8,128)} %fusion.183), kind=kCustom, calls=%fused_computation.2.clone.1 | custom fusion | flops 2097152 | bytes 25166848 | tf_op jit(solution)/shard_map/while/body/eval_jaxpr/scatter-add | solution.py:125
  396.4 29.5 %copy.85 = f32[4,128,2,64,64]{1,3,0,4,2:T(8,128)} copy(f32[4,128,2,64,64]{4,3,2,1,0:T(8,128)} %bitcast.124) | data formatting | bytes 33554432 | tf_op jit(solution)/shard_map/reshape | solution.py:129
  425.9 6.7 fusion.173
  432.6 9.4 fusion.51
  442.0 9.5 fusion.59
  451.5 9.3 fusion.53
  460.8 18.5 %fusion.8 = (f32[256,128,64]{1,0,2:T(8,128)}, f32[256,128,64]{1,0,2:T(8,128)}) fusion(f32[128,64]{0,1:T(8,128)S(1)} %copy-done.6, f32[128,64]{0,1:T(8,128)S(1)} %copy-done.7, f32[256,64,128]{2,0,1:T(8,128)} %fusion.51, f32[256,64,128]{2,0,1:T(8,128)} %fusion.59, f32[256,64,128]{2,0,1:T(8,128)} %fusion.53, f32[256,128,64]{1,0,2:T(8,128)} %bitcast.128), kind=kOutput, calls=%fused_computation.29 | convolution fusion | flops 3238232064 | bytes 50397184 | tf_op jit(solution)/shard_map/kq,rqp->rkp/dot_general | solution.py:16
  479.3 15.6 %fusion.28 = f32[64,256,128]{2,0,1:T(8,128)S(1)} fusion(f32[256,128,64]{1,0,2:T(8,128)} %get-tuple-element.119), kind=kOutput, calls=%fused_computation.57 | convolution fusion | flops 1610670080 | bytes 16777216 | tf_op jit(solution)/shard_map/rkp,pb->rbk/dot_general | solution.py:16
  494.9 17.3 %fusion.26 = f32[64,256,128]{2,0,1:T(8,128)} fusion(f32[256,128,64]{1,0,2:T(8,128)S(1)} %copy-done.2), kind=kOutput, calls=%fused_computation.55 | convolution fusion | flops 1610670080 | bytes 16777216 | tf_op jit(solution)/shard_map/rkp,pb->rbk/dot_general | solution.py:16
  512.2 17.5 %subtract_bitcast_fusion = f32[256,64,128]{2,1,0:T(8,128)} fusion(f32[64,256,128]{2,0,1:T(8,128)S(1)} %fusion.28, f32[256,128,64]{1,0,2:T(8,128)S(1)} %bitcast.130), kind=kOutput, calls=%fused_computation.38 | convolution fusion | flops 1612767232 | bytes 25165824 | tf_op jit(solution)/shard_map/rkp,pb->rbk/dot_general | solution.py:16
  529.7 9.4 stack_reshape.6
  539.1 18.0 %copy.90 = f32[1,256,8192]{1,0,2:T(1,128)} copy(f32[1,256,8192]{2,1,0:T(8,128)} %stack_reshape.6) | data formatting | bytes 16777216 | tf_op jit(solution)/shard_map/stack;reshape | solution.py:47
  557.1 18.9 %add_bitcast_fusion = f32[256,64,128]{2,1,0:T(8,128)} fusion(f32[64,256,128]{2,0,1:T(8,128)} %fusion.26, f32[256,128,64]{1,0,2:T(8,128)} %get-tuple-element.118), kind=kOutput, calls=%fused_computation.37 | convolution fusion | flops 1612767232 | bytes 25165824 | tf_op jit(solution)/shard_map/rkp,pb->rbk/dot_general | solution.py:16
  576.0 9.4 stack_reshape.7
  585.3 18.1 %copy.91 = f32[1,256,8192]{1,0,2:T(1,128)} copy(f32[1,256,8192]{2,1,0:T(8,128)} %stack_reshape.7) | data formatting | bytes 16777216 | tf_op jit(solution)/shard_map/stack;reshape | solution.py:47
  603.4 16.7 %pad_maximum_fusion = f32[2,256,8192]{1,0,2:T(2,128)S(1)} fusion(f32[1,256,8192]{1,0,2:T(1,128)} %copy.91, f32[1,256,8192]{1,0,2:T(1,128)} %copy.90), kind=kLoop, calls=%fused_computation.25 | loop fusion | flops 4194304 | bytes 33554432 | tf_op jit(solution)/shard_map/stack | solution.py:47
  620.1 371.7 %all_to_all.25 = f32[2,256,8192]{1,0,2:T(2,128)S(1)} all-to-all(f32[2,256,8192]{1,0,2:T(2,128)S(1)} %pad_maximum_fusion), channel_id=1, replica_groups=mesh['grp'=4,'dev'=8] {'grp','dev'}, dimensions={2} | all-to-all | bytes 33554432 | tf_op jit(solution)/shard_map/all_to_all | solution.py:132
  991.7 5.7 copy.92
  997.4 6.4 fusion.172
  1003.9 9.0 copy.93
  1012.9 17.5 %fusion.22 = f32[128,64,256]{2,0,1:T(8,128)} fusion(f32[128,64,256]{2,1,0:T(8,128)} %bitcast.131), kind=kOutput, calls=%fused_computation.51 | convolution fusion | flops 3221454848 | bytes 16777216 | tf_op jit(solution)/shard_map/bk,kpa->bpa/dot_general | solution.py:16
  1030.4 13.3 %fusion.24 = f32[128,64,256]{2,0,1:T(8,128)} fusion(f32[128,64,256]{2,1,0:T(8,128)S(1)} %bitcast.132), kind=kOutput, calls=%fused_computation.53 | convolution fusion | flops 3221454848 | bytes 16777216 | tf_op jit(solution)/shard_map/bk,kpa->bpa/dot_general | solution.py:16
  1043.8 9.0 copy.95
  1052.7 17.8 %fusion.20 = f32[128,64,256]{2,0,1:T(8,128)} fusion(f32[128,64,256]{2,1,0:T(8,128)} %bitcast.133), kind=kOutput, calls=%fused_computation.49 | convolution fusion | flops 3221454848 | bytes 16777216 | tf_op jit(solution)/shard_map/bk,kpa->bpa/dot_general | solution.py:16
  1070.6 20.2 %multiply_subtract_fusion = (f32[128,64,256]{2,0,1:T(8,128)S(1)}, f32[128,64,256]{2,0,1:T(8,128)S(1)}) fusion(f32[128,64]{0,1:T(8,128)S(1)} %copy-done.6, f32[128,64]{0,1:T(8,128)S(1)} %copy-done.7, f32[128,64,256]{2,0,1:T(8,128)} %fusion.22, f32[128,64,256]{2,0,1:T(8,128)} %fusion.24, f32[128,64,256]{2,0,1:T(8,128)} %fusion.20, f32[128,64,256]{2,1,0:T(8,128)} %bitcast.134), kind=kOutput, calls=%fused_computation.36 | convolution fusion | flops 3238232064 | bytes 50397184 | tf_op jit(solution)/shard_map/bk,kpa->bpa/dot_general | solution.py:16
  1090.8 13.4 %fusion.12 = f32[64,128,256]{2,0,1:T(8,128)} fusion(f32[128,64,256]{2,0,1:T(8,128)S(1)} %get-tuple-element.117), kind=kOutput, calls=%fused_computation.41 | convolution fusion | flops 1610670080 | bytes 16777216 | tf_op jit(solution)/shard_map/kpa,pb->abk/dot_general | solution.py:16
  1104.1 13.2 %fusion.10 = f32[64,128,256]{2,0,1:T(8,128)} fusion(f32[128,64,256]{2,0,1:T(8,128)S(1)} %get-tuple-element.117), kind=kOutput, calls=%fused_computation.39 | convolution fusion | flops 1610670080 | bytes 16777216 | tf_op jit(solution)/shard_map/kpa,pb->abk/dot_general | solution.py:16
  1117.3 15.9 %multiply_bitcast_fusion.1 = f32[256,64,128]{0,1,2:T(8,128)} fusion(f32[64,128,256]{2,0,1:T(8,128)} %fusion.12, f32[128,64,256]{2,0,1:T(8,128)S(1)} %get-tuple-element.116), kind=kOutput, calls=%fused_computation.34 | convolution fusion | flops 1614864384 | bytes 25165824 | tf_op jit(solution)/shard_map/kpa,pb->abk/dot_general | solution.py:16
  1133.2 11.6 copy.101
  1144.8 14.1 %multiply_bitcast_fusion = f32[256,64,128]{0,1,2:T(8,128)} fusion(f32[64,128,256]{2,0,1:T(8,128)S(1)} %copy-done.3, f32[128,64,256]{2,0,1:T(8,128)S(1)} %get-tuple-element.116), kind=kOutput, calls=%fused_computation.33 | convolution fusion | flops 1614864384 | bytes 25165824 | tf_op jit(solution)/shard_map/kpa,pb->abk/dot_general | solution.py:16
  1158.9 8.4 copy.104
  1167.3 6.0 pad_maximum_fusion.1
  1173.3 17.5 %copy.105 = f32[2,256,8192]{2,1,0:T(8,128)} copy(f32[2,256,8192]{1,2,0:T(8,128)} %pad_maximum_fusion.1) | data formatting | bytes 33554432 | tf_op jit(solution)/shard_map/stack | solution.py:69
  (67 shorter events, 3.7 us)
Async XLA Ops:
  7.2 58.0 %all-to-all-start = ((s32[32,32,3]{1,2,0:T(4,128)}), s32[32,32,3]{1,2,0:T(4,128)S(1)}, u32[]{:S(2)}, u32[]{:S(2)}) async-start(s32[32,32,3]{1,2,0:T(4,128)} %copy.83), calls=%async_computation | async-start | bytes 131072 | tf_op jit(solution)/shard_map/all_to_all | solution.py:96
  65.2 22.7 %all-to-all-start.1 = ((bf16[32,32,2,128]{3,2,1,0:T(2,128)(2,1)}), bf16[32,32,2,128]{3,2,1,0:T(2,128)(2,1)S(1)}, u32[]{:S(2)}, u32[]{:S(2)}) async-start(bf16[32,32,2,128]{3,2,1,0:T(2,128)(2,1)} %bitcast.16), calls=%async_computation.1 | async-start | bytes 1048576 | tf_op jit(solution)/shard_map/all_to_all | solution.py:89
  87.9 11.3 copy-start.5
  432.6 18.9 %copy-start = (f32[1,4,64,128,64]{3,2,1,4,0:T(8,128)}, f32[1,4,64,128,64]{3,2,1,4,0:T(8,128)S(1)}, u32[]{:S(2)}) copy-start(f32[1,4,64,128,64]{3,2,1,4,0:T(8,128)S(1)} %get-tuple-element.123) | copy-start | bytes 25165828
  451.5 9.3 copy-start.6
  451.5 9.3 copy-start.7
  479.3 15.7 %copy-start.2 = (f32[256,128,64]{1,0,2:T(8,128)S(1)}, f32[256,128,64]{1,0,2:T(8,128)}, u32[]{:S(2)}) copy-start(f32[256,128,64]{1,0,2:T(8,128)} %get-tuple-element.119) | copy-start | bytes 25165828
  479.3 32.9 %slice-start = ((s8[8388608]{0:T(1024)(128)(4,1)}), s8[4194304]{0:T(1024)(128)(4,1)S(1)}, s32[]{:S(2)}) async-start(s8[8388608]{0:T(1024)(128)(4,1)} %bitcast.129), calls=%async_computation.3 | async-start | bytes 8388608
  494.9 17.3 %slice-start.1 = ((s8[8388608]{0:T(1024)(128)(4,1)}), s8[4194304]{0:T(1024)(128)(4,1)S(1)}, s32[]{:S(2)}) async-start(s8[8388608]{0:T(1024)(128)(4,1)} %bitcast.129), calls=%async_computation.4 | async-start | bytes 8388608
  1012.9 17.5 %copy-start.1 = (f32[1,32,256,256]{3,2,1,0:T(8,128)S(1)}, f32[1,32,256,256]{3,2,1,0:T(8,128)}, u32[]{:S(2)}) copy-start(f32[1,32,256,256]{3,2,1,0:T(8,128)} %copy.93) | copy-start | bytes 25165828
  1133.2 11.6 copy-start.3
  1158.9 8.4 copy-start.4
where the time goes:
time: 1200 us; the launch traced here: 1190 us
  blocking collectives  372 us (31%)
  matrix products  283 us (24%)
  other arithmetic  258 us (22%)
  local copies, waits for them, and re-layouts  248 us (21%)
  waiting for transfers between devices  15.5 us (1%)
  starting transfers between devices  13.7 us (1%)
    all_to_all x1, blocking collectives, local(): lax.all_to_all(half, ('grp', 'dev'), split_axis=2, concat_axis=1, tiled=T...  372 us
    dot_general x16, matrix products, product(): return jnp.einsum(pattern, first, second, precision=lax.Precision.HIGHEST)  241 us
    scatter-add x4, other arithmetic, grid_block(): return uv_tiles.at[label_block[:, 0]].add(terms)  209 us
    another operation x4, local copies, waits for them, and re-layouts, along_rows(): jnp.stack([result_re.reshape(lines, GRID), result_im.reshape(lines, GRID)])  54.8 us
    scatter x1, local copies, waits for them, and re-layouts, local(): jnp.zeros((total_rows, 2, VIS), jnp.bfloat16).at[position].set(visibilities)  49.6 us
    dot_general x4, matrix products, grid_block(): jnp.einsum('rcik,rjk->rcij', weighted, right_kernel, preferred_element_ty...  41.5 us
    reshape x1, local copies, waits for them, and re-layouts, local(): uv_tiles.reshape(tile_rows, tile_cols, 2, TILE, TILE)  29.5 us
  transfers between devices with their start and end apart: 2, of which 1 were waited for; matrix products, arithmetic and copies ran while one was open for 4% of the time, Pallas kernels for 0%

commit v1 on v0

--- a/solution.py
+++ b/solution.py
@@ -129,7 +129,12 @@
     grid_rows = uv_tiles.reshape(tile_rows, tile_cols, 2, TILE, TILE).transpose(2, 0, 3, 1, 4)
     grid_rows = grid_rows.reshape(2, slab, GRID)
     half = along_rows(grid_rows)
-    columns = lax.all_to_all(half, ("grp", "dev"), split_axis=2, concat_axis=1, tiled=True)
+    columns = jnp.concatenate(
+        lax.all_to_all(
+            jnp.stack(jnp.split(half, lax.axis_size(("grp", "dev")), axis=2)), ("grp", "dev"), 0, 0
+        ),
+        axis=1,
+    )
     source_order = jnp.arange(QLEN, dtype=jnp.int32)
     return along_columns(columns, source_order)
 

time: 1200 us -> 1160 us (0.967)
  local copies, waits for them, and re-layouts: 248 us -> 230 us
  other arithmetic: 258 us -> 242 us
    another operation x4 -> x3, local copies, waits for them, and re-layouts: 54.8 us -> 22.7 us  [along_rows(): jnp.stack([result_re.reshape(lines, GRID), result_im.reshape(lines, GRID)])]
    unnamed x20 -> x52, local copies, waits for them, and re-layouts: 0.04 us -> 29.8 us
    another operation x3 -> x2, other arithmetic: 17.9 us -> 1.19 us  [the longest x1 16.7 us: along_rows(): jnp.stack([result_re.reshape(lines, GRID), result_im.reshape(lines, GRID)])]
where the time goes in v1:
time: 1160 us; the launch traced here: 1150 us
  blocking collectives  372 us (32%)
  matrix products  274 us (24%)
  other arithmetic  242 us (21%)
  local copies, waits for them, and re-layouts  230 us (20%)
  waiting for transfers between devices  15.5 us (1%)
  starting transfers between devices  13.7 us (1%)
    all_to_all x1, blocking collectives, local(): lax.all_to_all(jnp.stack(jnp.split(half, lax.axis_size(('grp', 'dev')), a...  372 us
    dot_general x16, matrix products, product(): return jnp.einsum(pattern, first, second, precision=lax.Precision.HIGHEST)  233 us
    scatter-add x4, other arithmetic, grid_block(): return uv_tiles.at[label_block[:, 0]].add(terms)  209 us
    scatter x1, local copies, waits for them, and re-layouts, local(): jnp.zeros((total_rows, 2, VIS), jnp.bfloat16).at[position].set(visibilities)  49.6 us
    dot_general x4, matrix products, grid_block(): jnp.einsum('rcik,rjk->rcij', weighted, right_kernel, preferred_element_ty...  41.5 us
    unnamed x52, local copies, waits for them, and re-layouts  29.8 us
    reshape x1, local copies, waits for them, and re-layouts, local(): uv_tiles.reshape(tile_rows, tile_cols, 2, TILE, TILE)  29.5 us
  transfers between devices with their start and end apart: 2, of which 1 were waited for; matrix products, arithmetic and copies ran while one was open for 4% of the time, Pallas kernels for 0%

profile of v1, /device:TPU:0, one launch (start us, length us, event | category | flops | bytes accessed | tf_op | source)
XLA Modules:
  0.0 1147.6 jit_solution(7824735748559662606)
XLA Ops:
  0.7 1.2 reduce-window.6
  4.5 1.8 scatter_custom_fusion.1
  6.3 0.9 copy.87
  7.2 7.3 all-to-all-start
  14.5 1.1 broadcast_in_dim.29
  15.5 49.6 %scatter_fusion.1 = bf16[1024,2,128]{2,1,0:T(2,128)(2,1)} fusion(bf16[1024,2,128]{2,1,0:T(2,128)(2,1)} %broadcast_in_dim.29, s32[512]{0:T(512)S(1)} %bitcast.277, bf16[512,2,128]{2,1,0:T(2,128)(2,1)} %param.9), kind=kCustom, calls=%fused_computation.4 | custom fusion | bytes 788480 | tf_op jit(solution)/shard_map/scatter | solution.py:85
  65.2 6.4 all-to-all-start.1
  72.4 15.5 %all-to-all-done.1 = bf16[32,32,2,128]{3,2,1,0:T(2,128)(2,1)S(1)} async-done(((bf16[32,32,2,128]{3,2,1,0:T(2,128)(2,1)}), bf16[32,32,2,128]{3,2,1,0:T(2,128)(2,1)S(1)}, u32[]{:S(2)}, u32[]{:S(2)}) %all-to-all-start.1) | async-done | bytes 524320 | tf_op jit(solution)/shard_map/all_to_all | solution.py:89
  87.9 11.2 broadcast_in_dim.26
  99.1 297.3 %while.13 = (s32[]{:T(128)}, f32[512,2,64,64]{3,2,1,0:T(8,128)}, s32[1024,3]{0,1:T(4,128)S(1)}, bf16[2,32,64,128]{3,2,1,0:T(8,128)(2,1)S(1)}, bf16[1024,2,128]{2...) while((s32[]{:T(128)}, f32[512,2,64,64]{3,2,1,0:T(8,128)}, ...), condition=%wide.region_7.9_spmd, body=%wide.region_5.0_spmd.sunk | while | flops 553721088 | bytes 78276800 | solution.py:128
  99.3 3.1 gather_fusion
  102.4 5.3 select_convert_fusion.2
  107.7 3.0 gather_fusion.1
  110.8 10.4 fusion.215
  121.2 52.2 %scatter_fusion = f32[512,2,64,64]{3,2,1,0:T(8,128)} fusion(f32[512,2,64,64]{3,2,1,0:T(8,128)} %get-tuple-element.179, s32[256]{0:T(256)S(1)} %bitcast.269, f32[256,2,64,64]{3,2,1,0:T(8,128)} %fusion.215), kind=kCustom, calls=%fused_computation.2.clone.1 | custom fusion | flops 2097152 | bytes 25166848 | tf_op jit(solution)/shard_map/while/body/eval_jaxpr/scatter-add | solution.py:125
  173.6 3.1 gather_fusion
  176.7 5.3 select_convert_fusion.2
  182.0 3.0 gather_fusion.1
  185.1 10.4 fusion.215
  195.5 52.3 %scatter_fusion = f32[512,2,64,64]{3,2,1,0:T(8,128)} fusion(f32[512,2,64,64]{3,2,1,0:T(8,128)} %get-tuple-element.179, s32[256]{0:T(256)S(1)} %bitcast.269, f32[256,2,64,64]{3,2,1,0:T(8,128)} %fusion.215), kind=kCustom, calls=%fused_computation.2.clone.1 | custom fusion | flops 2097152 | bytes 25166848 | tf_op jit(solution)/shard_map/while/body/eval_jaxpr/scatter-add | solution.py:125
  248.0 3.1 gather_fusion
  251.1 5.3 select_convert_fusion.2
  256.4 3.0 gather_fusion.1
  259.5 10.4 fusion.215
  269.9 52.2 %scatter_fusion = f32[512,2,64,64]{3,2,1,0:T(8,128)} fusion(f32[512,2,64,64]{3,2,1,0:T(8,128)} %get-tuple-element.179, s32[256]{0:T(256)S(1)} %bitcast.269, f32[256,2,64,64]{3,2,1,0:T(8,128)} %fusion.215), kind=kCustom, calls=%fused_computation.2.clone.1 | custom fusion | flops 2097152 | bytes 25166848 | tf_op jit(solution)/shard_map/while/body/eval_jaxpr/scatter-add | solution.py:125
  322.2 3.1 gather_fusion
  325.3 5.3 select_convert_fusion.2
  330.6 3.0 gather_fusion.1
  333.8 10.4 fusion.215
  344.1 52.3 %scatter_fusion = f32[512,2,64,64]{3,2,1,0:T(8,128)} fusion(f32[512,2,64,64]{3,2,1,0:T(8,128)} %get-tuple-element.179, s32[256]{0:T(256)S(1)} %bitcast.269, f32[256,2,64,64]{3,2,1,0:T(8,128)} %fusion.215), kind=kCustom, calls=%fused_computation.2.clone.1 | custom fusion | flops 2097152 | bytes 25166848 | tf_op jit(solution)/shard_map/while/body/eval_jaxpr/scatter-add | solution.py:125
  396.4 29.5 %copy.89 = f32[4,128,2,64,64]{1,3,0,4,2:T(8,128)} copy(f32[4,128,2,64,64]{4,3,2,1,0:T(8,128)} %bitcast.252) | data formatting | bytes 33554432 | tf_op jit(solution)/shard_map/reshape | solution.py:129
  425.9 6.7 fusion.205
  432.6 9.4 fusion.83
  442.0 9.5 fusion.91
  451.5 9.3 fusion.85
  460.8 18.5 %fusion.8 = (f32[256,128,64]{1,0,2:T(8,128)}, f32[256,128,64]{1,0,2:T(8,128)}) fusion(f32[128,64]{0,1:T(8,128)S(1)} %copy-done.6, f32[128,64]{0,1:T(8,128)S(1)} %copy-done.7, f32[256,64,128]{2,0,1:T(8,128)} %fusion.83, f32[256,64,128]{2,0,1:T(8,128)} %fusion.91, f32[256,64,128]{2,0,1:T(8,128)} %fusion.85, f32[256,128,64]{1,0,2:T(8,128)} %bitcast.256), kind=kOutput, calls=%fused_computation.29 | convolution fusion | flops 3238232064 | bytes 50397184 | tf_op jit(solution)/shard_map/kq,rqp->rkp/dot_general | solution.py:16
  479.3 15.7 %fusion.26 = f32[64,256,128]{2,0,1:T(8,128)S(1)} fusion(f32[256,128,64]{1,0,2:T(8,128)} %get-tuple-element.119), kind=kOutput, calls=%fused_computation.55 | convolution fusion | flops 1610670080 | bytes 16777216 | tf_op jit(solution)/shard_map/rkp,pb->rbk/dot_general | solution.py:16
  495.0 17.2 %fusion.28 = f32[64,256,128]{2,0,1:T(8,128)} fusion(f32[256,128,64]{1,0,2:T(8,128)S(1)} %copy-done.1), kind=kOutput, calls=%fused_computation.57 | convolution fusion | flops 1610670080 | bytes 16777216 | tf_op jit(solution)/shard_map/rkp,pb->rbk/dot_general | solution.py:16
  512.2 17.5 %add_bitcast_fusion = f32[256,64,128]{2,1,0:T(8,128)} fusion(f32[64,256,128]{2,0,1:T(8,128)S(1)} %fusion.26, f32[256,128,64]{1,0,2:T(8,128)S(1)} %bitcast.258), kind=kOutput, calls=%fused_computation.37 | convolution fusion | flops 1612767232 | bytes 25165824 | tf_op jit(solution)/shard_map/rkp,pb->rbk/dot_general | solution.py:16
  529.7 9.4 stack_reshape.7
  539.1 18.9 %subtract_bitcast_fusion = f32[256,64,128]{2,1,0:T(8,128)} fusion(f32[64,256,128]{2,0,1:T(8,128)} %fusion.28, f32[256,128,64]{1,0,2:T(8,128)} %get-tuple-element.118), kind=kOutput, calls=%fused_computation.38 | convolution fusion | flops 1612767232 | bytes 25165824 | tf_op jit(solution)/shard_map/rkp,pb->rbk/dot_general | solution.py:16
  558.0 9.4 stack_reshape.6
  567.4 3.9 constant_dynamic-update-slice_fusion.1
  571.3 4.0 constant_dynamic-update-slice_fusion
  575.3 0.8 fusion.73
  577.0 0.8 fusion.71
  580.3 0.8 fusion.67
  587.8 0.8 fusion.58
  591.1 0.8 fusion.54
  602.0 371.9 %all_to_all.15 = f32[32,2,256,256]{3,2,1,0:T(8,128)S(1)} all-to-all(f32[32,2,256,256]{3,2,1,0:T(8,128)} %fusion.42), channel_id=1, replica_groups=mesh['grp'=4,'dev'=8] {'grp','dev'}, dimensions={0} | all-to-all | bytes 33554432 | tf_op jit(solution)/shard_map/all_to_all | solution.py:133
  973.8 6.4 copy.144
  980.2 6.5 fusion.204
  986.8 13.1 %fusion.22 = f32[128,64,256]{2,0,1:T(8,128)} fusion(f32[128,64,256]{2,1,0:T(8,128)S(1)} %bitcast.259), kind=kOutput, calls=%fused_computation.51 | convolution fusion | flops 3221454848 | bytes 16777216 | tf_op jit(solution)/shard_map/bk,kpa->bpa/dot_general | solution.py:16
  999.9 13.5 %fusion.24 = f32[128,64,256]{2,0,1:T(8,128)} fusion(f32[128,64,256]{2,1,0:T(8,128)S(1)} %bitcast.260), kind=kOutput, calls=%fused_computation.53 | convolution fusion | flops 3221454848 | bytes 16777216 | tf_op jit(solution)/shard_map/bk,kpa->bpa/dot_general | solution.py:16
  1013.4 13.1 %fusion.20 = f32[128,64,256]{2,0,1:T(8,128)} fusion(f32[128,64,256]{2,1,0:T(8,128)S(1)} %bitcast.261), kind=kOutput, calls=%fused_computation.49 | convolution fusion | flops 3221454848 | bytes 16777216 | tf_op jit(solution)/shard_map/bk,kpa->bpa/dot_general | solution.py:16
  1026.6 20.4 %multiply_subtract_fusion = (f32[128,64,256]{2,0,1:T(8,128)S(1)}, f32[128,64,256]{2,0,1:T(8,128)S(1)}) fusion(f32[128,64]{0,1:T(8,128)S(1)} %copy-done.6, f32[128,64]{0,1:T(8,128)S(1)} %copy-done.7, f32[128,64,256]{2,0,1:T(8,128)} %fusion.22, f32[128,64,256]{2,0,1:T(8,128)} %fusion.24, f32[128,64,256]{2,0,1:T(8,128)} %fusion.20, f32[128,64,256]{2,1,0:T(8,128)} %bitcast.262), kind=kOutput, calls=%fused_computation.36 | convolution fusion | flops 3238232064 | bytes 50397184 | tf_op jit(solution)/shard_map/bk,kpa->bpa/dot_general | solution.py:16
  1046.9 13.2 %fusion.12 = f32[64,128,256]{2,0,1:T(8,128)} fusion(f32[128,64,256]{2,0,1:T(8,128)S(1)} %get-tuple-element.117), kind=kOutput, calls=%fused_computation.41 | convolution fusion | flops 1610670080 | bytes 16777216 | tf_op jit(solution)/shard_map/kpa,pb->abk/dot_general | solution.py:16
  1060.1 13.4 %fusion.10 = f32[64,128,256]{2,0,1:T(8,128)} fusion(f32[128,64,256]{2,0,1:T(8,128)S(1)} %get-tuple-element.117), kind=kOutput, calls=%fused_computation.39 | convolution fusion | flops 1610670080 | bytes 16777216 | tf_op jit(solution)/shard_map/kpa,pb->abk/dot_general | solution.py:16
  1073.5 15.9 %multiply_bitcast_fusion.1 = f32[256,64,128]{0,1,2:T(8,128)} fusion(f32[64,128,256]{2,0,1:T(8,128)} %fusion.12, f32[128,64,256]{2,0,1:T(8,128)S(1)} %get-tuple-element.116), kind=kOutput, calls=%fused_computation.34 | convolution fusion | flops 1614864384 | bytes 25165824 | tf_op jit(solution)/shard_map/kpa,pb->abk/dot_general | solution.py:16
  1089.4 11.6 %copy.101 = f32[256,64,128]{0,2,1:T(8,128)} copy(f32[256,64,128]{0,1,2:T(8,128)} %multiply_bitcast_fusion.1) | data formatting | bytes 16777216 | tf_op jit(solution)/shard_map/mul | solution.py:70
  1101.1 14.1 %multiply_bitcast_fusion = f32[256,64,128]{0,1,2:T(8,128)} fusion(f32[64,128,256]{2,0,1:T(8,128)S(1)} %copy-done.3, f32[128,64,256]{2,0,1:T(8,128)S(1)} %get-tuple-element.116), kind=kOutput, calls=%fused_computation.33 | convolution fusion | flops 1614864384 | bytes 25165824 | tf_op jit(solution)/shard_map/kpa,pb->abk/dot_general | solution.py:16
  1115.2 8.4 copy.104
  1123.6 6.0 pad_maximum_fusion
  1129.6 17.5 %copy.105 = f32[2,256,8192]{2,1,0:T(8,128)} copy(f32[2,256,8192]{1,2,0:T(8,128)} %pad_maximum_fusion) | data formatting | bytes 33554432 | tf_op jit(solution)/shard_map/stack | solution.py:69
  (96 shorter events, 27.8 us)
Async XLA Ops:
  7.2 58.0 %all-to-all-start = ((s32[32,32,3]{1,2,0:T(4,128)}), s32[32,32,3]{1,2,0:T(4,128)S(1)}, u32[]{:S(2)}, u32[]{:S(2)}) async-start(s32[32,32,3]{1,2,0:T(4,128)} %copy.87), calls=%async_computation | async-start | bytes 131072 | tf_op jit(solution)/shard_map/all_to_all | solution.py:96
  65.2 22.7 %all-to-all-start.1 = ((bf16[32,32,2,128]{3,2,1,0:T(2,128)(2,1)}), bf16[32,32,2,128]{3,2,1,0:T(2,128)(2,1)S(1)}, u32[]{:S(2)}, u32[]{:S(2)}) async-start(bf16[32,32,2,128]{3,2,1,0:T(2,128)(2,1)} %bitcast.16), calls=%async_computation.1 | async-start | bytes 1048576 | tf_op jit(solution)/shard_map/all_to_all | solution.py:89
  87.9 11.3 copy-start.5
  432.6 18.9 %copy-start = (f32[1,4,64,128,64]{3,2,1,4,0:T(8,128)}, f32[1,4,64,128,64]{3,2,1,4,0:T(8,128)S(1)}, u32[]{:S(2)}) copy-start(f32[1,4,64,128,64]{3,2,1,4,0:T(8,128)S(1)} %get-tuple-element.123) | copy-start | bytes 25165828
  451.5 9.3 copy-start.6
  451.5 9.3 copy-start.7
  479.3 15.7 %copy-start.1 = (f32[256,128,64]{1,0,2:T(8,128)S(1)}, f32[256,128,64]{1,0,2:T(8,128)}, u32[]{:S(2)}) copy-start(f32[256,128,64]{1,0,2:T(8,128)} %get-tuple-element.119) | copy-start | bytes 25165828
  479.3 33.0 %slice-start = ((s8[8388608]{0:T(1024)(128)(4,1)}), s8[4194304]{0:T(1024)(128)(4,1)S(1)}, s32[]{:S(2)}) async-start(s8[8388608]{0:T(1024)(128)(4,1)} %bitcast.257), calls=%async_computation.3 | async-start | bytes 8388608
  495.0 17.3 %slice-start.1 = ((s8[8388608]{0:T(1024)(128)(4,1)}), s8[4194304]{0:T(1024)(128)(4,1)S(1)}, s32[]{:S(2)}) async-start(s8[8388608]{0:T(1024)(128)(4,1)} %bitcast.257), calls=%async_computation.4 | async-start | bytes 8388608
  986.8 26.6 %copy-start.2 = (f32[1,32,256,256]{3,2,1,0:T(8,128)}, f32[1,32,256,256]{3,2,1,0:T(8,128)S(1)}, u32[]{:S(2)}) copy-start(f32[1,32,256,256]{3,2,1,0:T(8,128)S(1)} %get-tuple-element.121) | copy-start | bytes 25165828
  1089.4 11.6 %copy-start.3 = (f32[64,128,256]{2,0,1:T(8,128)S(1)}, f32[64,128,256]{2,0,1:T(8,128)}, u32[]{:S(2)}) copy-start(f32[64,128,256]{2,0,1:T(8,128)} %fusion.10) | copy-start | bytes 25165828
  1115.2 8.4 copy-start.4
